TPU v7x, 32 devices: a whole 2x2x4 slice. The times are simulated.
32 devices in a mesh: band: 4 (over y, x), slab: 8 (over z, core).
Axes of the slice: x: 2, y: 2, z: 4, core: 2. Of those that a mesh axis runs over, the one named last changes fastest.
Arguments:
- band_block: float32 [4, 2, 2, 128, 128, 128], P(None, None, None, 'band', 'slab'), may hold values from -24 to 24
- material_grid: int32 [128, 128, 128], P('slab'), may hold values from 0 to 3
- inverse_permittivity: float32 [4], replicated, may hold values from 0.077 to 1
- bloch_index: int32 [1], replicated, may hold values from 0 to 7
Outputs:
- search_block: float32 [4, 2, 2, 128, 128, 128], P(None, None, None, 'band', 'slab')
- correlation: float32 [2, 8, 8], replicated
- projected: float32 [2, 8, 8], replicated
All inputs are finite; a program needn't handle non-finite values.
Results may differ from a plain program's by a relative error of at most 0.00005.
Values sent between devices are 32-bit elements; how exact they have to be, the bound alone decides.
A program may use at most 192 MiB of HBM per device.

v0:
```python
from functools import partial
import math

import jax
import jax.numpy as jnp
from jax import lax
from jax.sharding import PartitionSpec as P

KPOINTS = 8


HIGHEST = lax.Precision.HIGHEST


def axis_values(length, weight, fraction, offset, extent):
    indices = offset + jnp.arange(extent, dtype=jnp.int32)
    signed = jnp.where(indices >= length // 2, indices - length, indices).astype(jnp.float32)
    return 2.0 * math.pi / length * (signed + weight * fraction)


def frame(depth_wave, height_wave, width_wave):
    depth_term = depth_wave[:, None, None]
    height_term = height_wave[None, :, None]
    width_term = width_wave[None, None, :]
    planar = jnp.sqrt(width_term * width_term + height_term * height_term)
    magnitude = jnp.sqrt(planar * planar + depth_term * depth_term)
    grid_shape = magnitude.shape
    primary = [
        jnp.broadcast_to(height_term / planar, grid_shape),
        jnp.broadcast_to(-width_term / planar, grid_shape),
        jnp.zeros(grid_shape, magnitude.dtype),
    ]
    secondary = [
        width_term * depth_term / (magnitude * planar),
        height_term * depth_term / (magnitude * planar),
        -planar / magnitude,
    ]
    return (primary, secondary, magnitude)


def curl_field(block, primary, secondary, magnitude):
    first_comp = block[:, 0]
    second_comp = block[:, 1]
    parts = [
        magnitude * (first_comp * secondary[component] - second_comp * primary[component])
        for component in range(3)
    ]
    return jnp.stack(parts, axis=1).reshape((-1,) + first_comp.shape[1:])


def project_back(spectrum, primary, secondary, magnitude, band_count):
    grouped = spectrum.reshape((band_count, 3) + spectrum.shape[1:])
    along_second = (
        grouped[:, 0] * secondary[0] + grouped[:, 1] * secondary[1] + grouped[:, 2] * secondary[2]
    )
    along_primary = (
        grouped[:, 0] * primary[0] + grouped[:, 1] * primary[1] + grouped[:, 2] * primary[2]
    )
    return jnp.stack([magnitude * along_second, -magnitude * along_primary], axis=1)


def transform(values, target, direction):
    length = values.shape[target]
    indices = jnp.arange(length, dtype=jnp.int32)
    products = indices[:, None] * indices[None, :] % length
    angles = 2.0 * math.pi / length * products.astype(jnp.float32)
    cosine = jnp.cos(angles)
    sine_table = direction * jnp.sin(angles)
    letters = "abc"
    source = letters[target - 2]
    formula = "i" + letters + "," + source + "w" + "->" + "i" + letters.replace(source, "w")
    contract = partial(jnp.einsum, formula, precision=HIGHEST)
    real_part = values[:, 0]
    imaginary = values[:, 1]
    new_real = contract(real_part, cosine) - contract(imaginary, sine_table)
    new_imag = contract(real_part, sine_table) + contract(imaginary, cosine)
    return jnp.stack([new_real, new_imag], axis=1)


def cell_values(material_grid, inverse_permittivity, grid_cells):
    inverse_cells = jnp.zeros(material_grid.shape, jnp.float32)
    for material in range(inverse_permittivity.shape[0]):
        inverse_cells = inverse_cells + jnp.where(
            material_grid == material, inverse_permittivity[material], 0.0
        )
    return inverse_cells / grid_cells


def gram_parts(left, right):
    left_real = left[:, :, 0].reshape(left.shape[0], -1)
    left_imag = left[:, :, 1].reshape(left.shape[0], -1)
    right_real = right[:, :, 0].reshape(right.shape[0], -1)
    right_imag = right[:, :, 1].reshape(right.shape[0], -1)
    inner_product = partial(jnp.einsum, "km,jm->kj", precision=HIGHEST)
    real_sum = inner_product(left_real, right_real) + inner_product(left_imag, right_imag)
    imag_sum = inner_product(left_real, right_imag) - inner_product(left_imag, right_real)
    return (real_sum, imag_sum)


def shards(band_block, material_grid, inverse_permittivity, bloch_index):
    band_groups = lax.axis_size("band")
    slab_count = lax.axis_size("slab")
    band_count = band_block.shape[0]
    depth_share = band_block.shape[3]
    row_share = band_block.shape[4]
    line_length = band_block.shape[5]
    full_depth = depth_share * band_groups
    full_rows = row_share * slab_count
    grid_cells = full_depth * full_rows * line_length
    fraction = (bloch_index[0].astype(jnp.float32) + 1.0) / KPOINTS
    row_offset = lax.axis_index("slab") * row_share
    depth_offset = lax.axis_index("band") * depth_share
    width_wave = axis_values(line_length, 0.5, fraction, 0, line_length)
    row_wave = axis_values(full_rows, 0.35, fraction, row_offset, row_share)
    point_frame = frame(
        axis_values(full_depth, 0.2, fraction, depth_offset, depth_share), row_wave, width_wave
    )
    inverse_cells = cell_values(material_grid, inverse_permittivity, grid_cells)

    def slab_operator(points):
        gathered = lax.all_to_all(points, "band", split_axis=0, concat_axis=3, tiled=True)
        primary, secondary, magnitude = frame(
            axis_values(full_depth, 0.2, fraction, 0, full_depth), row_wave, width_wave
        )
        curled = curl_field(gathered, primary, secondary, magnitude)
        spectrum = transform(transform(curled, 4, 1.0), 2, 1.0)
        spatial = (
            transform(
                lax.all_to_all(spectrum, "slab", split_axis=2, concat_axis=3, tiled=True), 3, 1.0
            )
            * inverse_cells[None, None]
        )
        returned = lax.all_to_all(
            transform(spatial, 3, -1.0), "slab", split_axis=3, concat_axis=2, tiled=True
        )
        finished = transform(transform(returned, 2, -1.0), 4, -1.0)
        local_image = project_back(finished, primary, secondary, magnitude, gathered.shape[0])
        return lax.all_to_all(local_image, "band", split_axis=3, concat_axis=0, tiled=True)

    def apply_operator(points):
        return slab_operator(points)

    image = apply_operator(band_block)
    correlation_real, correlation_imag = gram_parts(band_block, band_block)
    cross_real, cross_imag = gram_parts(band_block, image)
    correlation_real, correlation_imag, cross_real, cross_imag = lax.psum(
        (correlation_real, correlation_imag, cross_real, cross_imag), ("band", "slab")
    )
    correlation_real = correlation_real / grid_cells
    correlation_imag = correlation_imag / grid_cells
    cross_real = cross_real / grid_cells
    cross_imag = cross_imag / grid_cells
    system = jnp.concatenate(
        [
            jnp.concatenate([correlation_real, -correlation_imag], 1),
            jnp.concatenate([correlation_imag, correlation_real], 1),
        ],
        0,
    )
    right_side = jnp.concatenate([cross_real, cross_imag], 0)
    factor = jnp.linalg.cholesky(system)
    solution = jax.scipy.linalg.cho_solve((factor, True), right_side)
    mixing_real = solution[:band_count]
    mixing_imag = solution[band_count:]
    block_real = band_block[:, :, 0]
    block_imag = band_block[:, :, 1]
    combine = partial(jnp.einsum, "iabcd,ij->jabcd", precision=HIGHEST)
    residual_real = image[:, :, 0] - (
        combine(block_real, mixing_real) - combine(block_imag, mixing_imag)
    )
    residual_imag = image[:, :, 1] - (
        combine(block_real, mixing_imag) + combine(block_imag, mixing_real)
    )
    magnitude = point_frame[2]
    search_block = jnp.stack([residual_real, residual_imag], axis=2) / (magnitude * magnitude + 1.0)
    search_image = apply_operator(search_block)
    stacked = jnp.concatenate([band_block, search_block], 0)
    joint_real, joint_imag = gram_parts(stacked, search_block)
    image_real, image_imag = gram_parts(stacked, search_image)
    back_real, back_imag = gram_parts(search_block, image)
    joint_real, joint_imag, image_real, image_imag, back_real, back_imag = lax.psum(
        (joint_real, joint_imag, image_real, image_imag, back_real, back_imag), ("band", "slab")
    )
    joint_real = joint_real / grid_cells
    joint_imag = joint_imag / grid_cells
    image_real = image_real / grid_cells
    image_imag = image_imag / grid_cells
    back_real = back_real / grid_cells
    back_imag = back_imag / grid_cells
    upper_real = jnp.concatenate([correlation_real, joint_real[:band_count]], 1)
    lower_real = jnp.concatenate([joint_real[:band_count].T, joint_real[band_count:]], 1)
    upper_imag = jnp.concatenate([correlation_imag, joint_imag[:band_count]], 1)
    lower_imag = jnp.concatenate([-joint_imag[:band_count].T, joint_imag[band_count:]], 1)
    correlation = jnp.stack(
        [
            jnp.concatenate([upper_real, lower_real], 0),
            jnp.concatenate([upper_imag, lower_imag], 0),
        ],
        0,
    )
    top_real = jnp.concatenate([cross_real, image_real[:band_count]], 1)
    bottom_real = jnp.concatenate([back_real, image_real[band_count:]], 1)
    top_imag = jnp.concatenate([cross_imag, image_imag[:band_count]], 1)
    bottom_imag = jnp.concatenate([back_imag, image_imag[band_count:]], 1)
    projected = jnp.stack(
        [jnp.concatenate([top_real, bottom_real], 0), jnp.concatenate([top_imag, bottom_imag], 0)],
        0,
    )
    return (search_block, correlation, projected)


def solution(mesh):
    return jax.shard_map(
        shards,
        mesh=mesh,
        in_specs=(P(None, None, None, "band", "slab", None), P("slab", None, None), P(), P()),
        out_specs=(P(None, None, None, "band", "slab", None), P(), P()),
        check_vma=False,
    )
```

profile of v0, /device:TPU:10, one launch (start us, length us, event | category | flops | bytes accessed | tf_op | source)
XLA Modules:
  0.0 1215.9 jit_solution(13152435408415823991)
XLA Ops:
  0.6 5.4 all-to-all-start
  9.0 44.1 %all-to-all-done = f32[4,2,2,32,16,128]{5,4,3,2,1,0:T(8,128)} async-done(((f32[4,2,2,32,16,128]{5,4,3,2,1,0:T(8,128)}), f32[4,2,2,32,16,128]{5,4,3,2,1,0:T(8,128)}, u32[]{:S(2)}, u32[]{:S(2)}) %all-to-all-start) | async-done | bytes 4194336 | tf_op jit(solution)/shard_map/all_to_all | solution.py:121
  53.1 3.6 copy.132
  77.1 3.5 subtract_bitcast_fusion.7
  84.6 6.3 copy.137
  90.9 5.8 all-to-all-start.1
  97.4 5.2 add_multiply_fusion.4
  102.6 129.2 %all-to-all-done.1 = f32[3,2,128,16,128]{4,3,0,1,2:T(8,128)} async-done(((f32[3,2,128,16,128]{4,3,0,1,2:T(8,128)}), f32[3,2,128,16,128]{4,3,0,1,2:T(8,128)}, u32[]{:S(2)}, u32[]{:S(2)}) %all-to-all-start.1) | async-done | bytes 6291488 | tf_op jit(solution)/shard_map/all_to_all | solution.py:129
  231.8 3.7 copy.138
  242.0 3.4 subtract_bitcast_fusion.6
  245.4 3.6 add_bitcast_fusion.6
  256.8 3.4 subtract_bitcast_fusion.5
  260.1 3.6 add_bitcast_fusion.5
  264.5 3.6 copy.147
  268.1 142.7 %all_to_all.144 = f32[3,2,16,128,128]{4,2,0,1,3:T(8,128)S(1)} all-to-all(f32[3,2,16,128,128]{4,2,0,1,3:T(8,128)S(1)} %copy.147), channel_id=1, replica_groups=mesh['band'=4,'slab'=8] {'slab'}, dimensions={3} | all-to-all | bytes 12582912 | tf_op jit(solution)/shard_map/all_to_all | solution.py:133
  427.7 3.3 fusion.55
  434.0 3.4 add_bitcast_fusion.4
  440.7 4.5 copy.153
  445.1 5.4 all-to-all-start.3
  450.5 6.9 copy.156
  457.4 11.8 convolution_bitcast_fusion.6
  469.2 11.8 fusion.95
  481.0 9.1 convolution_bitcast_fusion.4
  490.2 9.3 fusion.96
  499.5 5.0 copy.305
  504.6 9.7 convolution_bitcast_fusion.2
  514.3 9.3 convolution_bitcast_fusion
  523.5 9.7 fusion.98
  533.2 9.3 fusion.100
  542.7 42.0 %all-reduce.1 = (f32[4,4]{0,1:T(4,128)S(1)}, f32[4,4]{0,1:T(4,128)S(1)}, f32[4,4]{0,1:T(4,128)S(1)}, f32[4,4]{0,1:T(4,128)S(1)}) all-reduce(f32[4,4]{0,1:T(4,128)S(1)} %fusion.95, f32[4,4]{0,1:T(4,128)S(1)} %fusion.96, f32[4,4]{0,1:T(4,128)S(1)} %fusion.100, f32[4,4]{0,1:T(4,128)S(1)} %fusion.98), channel_id=1, replica_groups=mesh['band'=4,'slab'=8] {'band','slab'}, use_global_device_ids=true, to_apply=%region_0.1 | all-reduce | flops 64 | bytes 512 | tf_op jit(solution)/shard_map/psum | solution.py:146
  588.4 5.8 fusion.106
  594.2 3.8 fusion.105
  598.0 4.1 subtract_bitcast_fusion.9
  602.1 4.0 subtract_bitcast_fusion.8
  610.0 49.0 %all_to_all.145 = f32[4,2,2,32,16,128]{5,4,3,1,2,0:T(8,128)S(1)} all-to-all(f32[4,2,2,32,16,128]{5,4,3,1,2,0:T(8,128)S(1)} %copy.169), channel_id=1, replica_groups=mesh['band'=4,'slab'=8] {'band'}, dimensions={0} | all-to-all | bytes 8388608 | tf_op jit(solution)/shard_map/all_to_all | solution.py:121
  670.7 3.4 fusion.140
  680.4 3.3 subtract_bitcast_fusion.3
  683.6 3.5 add_bitcast_fusion.3
  687.7 3.6 copy.175
  691.3 139.8 %all_to_all.146 = f32[3,2,128,16,128]{4,3,0,1,2:T(8,128)S(1)} all-to-all(f32[3,2,128,16,128]{4,3,0,1,2:T(8,128)S(1)} %copy.175), channel_id=1, replica_groups=mesh['band'=4,'slab'=8] {'slab'}, dimensions={2} | all-to-all | bytes 12582912 | tf_op jit(solution)/shard_map/all_to_all | solution.py:129
  838.6 3.3 subtract_bitcast_fusion.2
  841.9 3.6 add_bitcast_fusion.2
  852.8 3.3 subtract_bitcast_fusion.1
  856.1 3.7 add_bitcast_fusion.1
  860.3 3.6 copy.185
  863.9 141.4 %all_to_all.147 = f32[3,2,16,128,128]{4,2,0,1,3:T(8,128)S(1)} all-to-all(f32[3,2,16,128,128]{4,2,0,1,3:T(8,128)S(1)} %copy.185), channel_id=1, replica_groups=mesh['band'=4,'slab'=8] {'slab'}, dimensions={3} | all-to-all | bytes 12582912 | tf_op jit(solution)/shard_map/all_to_all | solution.py:133
  1022.2 3.3 fusion.51
  1028.5 3.4 add_bitcast_fusion
  1034.9 4.4 copy.191
  1039.2 5.9 all-to-all-start.7
  1045.1 11.8 fusion.87
  1056.9 11.0 fusion.88
  1070.2 9.4 fusion.102
  1079.6 9.5 fusion.101
  1089.2 9.1 fusion.79
  1098.3 9.3 fusion.80
  1107.6 9.5 fusion.94
  1117.1 9.3 fusion.93
  1126.4 5.0 copy.304
  1131.5 9.1 fusion.83
  1140.6 9.6 fusion.84
  1150.2 9.5 fusion.92
  1159.8 9.3 fusion.91
  1171.6 41.8 %all-reduce = (f32[8,4]{0,1:T(4,128)S(1)}, f32[8,4]{0,1:T(4,128)S(1)}, f32[8,4]{0,1:T(4,128)S(1)}, f32[4,4]{0,1:T(4,128)S(1)}, f32[8,4]{0,1:T(4,128)S(1)}, /*index=5*/f32[4,4]{0,1:T(4,128)S(1)}) all-reduce(f32[8,4]{0,1:T(4,128)S(1)} %fusion.93, f32[8,4]{0,1:T(4,128)S(1)} %fusion.94, ...), channel_id=1, replica_groups=mesh['band'=4,'slab'=8] {'band','slab'}, use_global_device_ids=true, to_apply=%region_7.8 | all-reduce | flops 160 | bytes 1280 | tf_op jit(solution)/shard_map/psum | solution.py:181
  (165 shorter events, 136.5 us)
Async XLA Ops:
  0.6 52.5 %all-to-all-start = ((f32[4,2,2,32,16,128]{5,4,3,2,1,0:T(8,128)}), f32[4,2,2,32,16,128]{5,4,3,2,1,0:T(8,128)}, u32[]{:S(2)}, u32[]{:S(2)}) async-start(f32[4,2,2,32,16,128]{5,4,3,2,1,0:T(8,128)} %param.4), calls=%async_computation | async-start | bytes 8388608 | tf_op jit(solution)/shard_map/all_to_all | solution.py:121
  53.1 3.6 copy-start.14
  90.9 5.8 copy-start.29
  90.9 140.9 %all-to-all-start.1 = ((f32[3,2,128,16,128]{4,3,0,1,2:T(8,128)}), f32[3,2,128,16,128]{4,3,0,1,2:T(8,128)}, u32[]{:S(2)}, u32[]{:S(2)}) async-start(f32[3,2,128,16,128]{4,3,0,1,2:T(8,128)} %copy.137), calls=%async_computation.1 | async-start | bytes 12582912 | tf_op jit(solution)/shard_map/all_to_all | solution.py:129
  245.4 3.6 copy-start.19
  437.4 1.2 copy-start.15
  437.4 1.5 copy-start.17
  445.1 54.4 %all-to-all-start.3 = ((f32[1,2,2,128,16,128]{5,4,1,2,0,3:T(8,128)}), f32[1,2,2,128,16,128]{5,4,1,2,0,3:T(8,128)}, u32[]{:S(2)}, u32[]{:S(2)}) async-start(f32[1,2,2,128,16,128]{5,4,1,2,0,3:T(8,128)} %copy.153), calls=%async_computation.3 | async-start | bytes 8388608 | tf_op jit(solution)/shard_map/all_to_all | solution.py:138
  457.4 23.6 %copy-start = (f32[4,2,2,32,16,128]{5,0,4,3,1,2:T(4,128)S(1)}, f32[4,2,2,32,16,128]{5,0,4,3,1,2:T(4,128)}, u32[]{:S(2)}) copy-start(f32[4,2,2,32,16,128]{5,0,4,3,1,2:T(4,128)} %copy.156) | copy-start | bytes 12582916
  499.5 5.1 copy-start.1
  504.6 28.6 %copy-start.7 = (f32[1,2,2,4,32,16,128]{6,3,5,4,1,2,0:T(4,128)}, f32[1,2,2,4,32,16,128]{6,3,5,4,1,2,0:T(4,128)S(1)}, u32[]{:S(2)}) copy-start(f32[1,2,2,4,32,16,128]{6,3,5,4,1,2,0:T(4,128)S(1)} %copy.305) | copy-start | bytes 12582916
  584.6 13.3 %copy-start.21 = (f32[4,4]{0,1:T(4,128)}, f32[4,4]{0,1:T(4,128)S(1)}, u32[]{:S(2)}) copy-start(f32[4,4]{0,1:T(4,128)S(1)} %get-tuple-element.54) | copy-start | bytes 196
  584.7 13.4 %copy-start.23 = (f32[4,4]{0,1:T(4,128)}, f32[4,4]{0,1:T(4,128)S(1)}, u32[]{:S(2)}) copy-start(f32[4,4]{0,1:T(4,128)S(1)} %broadcast_multiply_fusion.24) | copy-start | bytes 196
  587.7 6.5 copy-start.2
  587.7 0.6 copy-start.25
  587.7 0.6 copy-start.27
  594.2 3.8 copy-start.8
  607.9 2.0 copy-start.4
  659.0 1.3 copy-start.16
  841.9 3.6 copy-start.20
  1031.9 1.2 copy-start.18
  1039.2 87.2 %all-to-all-start.7 = ((f32[1,2,2,128,16,128]{5,4,1,2,0,3:T(8,128)}), f32[1,2,2,128,16,128]{5,4,1,2,0,3:T(8,128)}, u32[]{:S(2)}, u32[]{:S(2)}) async-start(f32[1,2,2,128,16,128]{5,4,1,2,0,3:T(8,128)} %copy.191), calls=%async_computation.7 | async-start | bytes 8388608 | tf_op jit(solution)/shard_map/all_to_all | solution.py:138
  1045.1 11.8 copy-start.5
  1056.9 11.0 copy-start.3
  1067.9 2.2 copy-start.9
  1070.2 37.4 %copy-start.12 = (f32[8,2,32,16,128]{4,0,3,2,1:T(8,128)}, f32[8,2,32,16,128]{4,0,3,2,1:T(8,128)S(1)}, u32[]{:S(2)}) copy-start(f32[8,2,32,16,128]{4,0,3,2,1:T(8,128)S(1)} %get-tuple-element.25) | copy-start | bytes 12582916
  1070.2 46.9 %copy-start.10 = (f32[8,2,32,16,128]{4,0,3,2,1:T(8,128)}, f32[8,2,32,16,128]{4,0,3,2,1:T(8,128)S(1)}, u32[]{:S(2)}) copy-start(f32[8,2,32,16,128]{4,0,3,2,1:T(8,128)S(1)} %get-tuple-element.24) | copy-start | bytes 12582916
  1126.4 5.1 copy-start.11
  1131.5 9.1 copy-start.13
  1159.8 9.3 copy-start.6
  1169.1 44.4 %copy-start.28 = (f32[4,4]{0,1:T(4,128)S(1)}, f32[4,4]{0,1:T(4,128)}, u32[]{:S(2)}) copy-start(f32[4,4]{0,1:T(4,128)} %copy-done.27) | copy-start | bytes 196
  1169.1 44.6 %copy-start.26 = (f32[4,4]{0,1:T(4,128)S(1)}, f32[4,4]{0,1:T(4,128)}, u32[]{:S(2)}) copy-start(f32[4,4]{0,1:T(4,128)} %copy-done.25) | copy-start | bytes 196
  1169.1 44.9 %copy-start.24 = (f32[4,4]{0,1:T(4,128)S(1)}, f32[4,4]{0,1:T(4,128)}, u32[]{:S(2)}) copy-start(f32[4,4]{0,1:T(4,128)} %copy-done.23) | copy-start | bytes 196
  1169.1 45.2 %copy-start.22 = (f32[4,4]{0,1:T(4,128)S(1)}, f32[4,4]{0,1:T(4,128)}, u32[]{:S(2)}) copy-start(f32[4,4]{0,1:T(4,128)} %copy-done.21) | copy-start | bytes 196
where the time goes:
time: 1230 us; the launch traced here: 1220 us
  blocking collectives  557 us (45%)
  matrix products  369 us (30%)
  waiting for transfers between devices  173 us (14%)
  local copies, waits for them, and re-layouts  62.4 us (5%)
  other arithmetic  29 us (2%)
  starting transfers between devices  22.5 us (2%)
    all_to_all x2, blocking collectives, slab_operator(): lax.all_to_all(transform(spatial, 3, -1.0), 'slab', split_axis=3, concat_...  284 us
    all_to_all x1, blocking collectives, slab_operator(): lax.all_to_all(spectrum, 'slab', split_axis=2, concat_axis=3, tiled=True)  140 us
    all_to_all x1, waiting for transfers between devices, slab_operator(): lax.all_to_all(spectrum, 'slab', split_axis=2, concat_axis=3, tiled=True)  129 us
    dot_general x24, matrix products, transform(): new_imag = contract(real_part, sine_table) + contract(imaginary, cosine)  78.1 us
    dot_general x24, matrix products, transform(): new_real = contract(real_part, cosine) - contract(imaginary, sine_table)  76.9 us
    dot_general x5, matrix products, gram_parts(): inner_product(left_imag, right_imag)  51.4 us
    dot_general x5, matrix products, gram_parts(): inner_product(left_real, right_real) + inner_product(left_imag, right_imag)  49.9 us
    all_to_all x1, blocking collectives, slab_operator(): lax.all_to_all(points, 'band', split_axis=0, concat_axis=3, tiled=True)  49 us
  transfers between devices with their start and end apart: 4, of which 2 were waited for; matrix products, arithmetic and copies ran while one was open for 11% of the time, Pallas kernels for 0%

commit v1 on v0

--- a/solution.py
+++ b/solution.py
@@ -4,6 +4,8 @@
 import jax
 import jax.numpy as jnp
 from jax import lax
+from jax.experimental import pallas as pl
+from jax.experimental.pallas import tpu as pltpu
 from jax.sharding import PartitionSpec as P
 
 KPOINTS = 8
@@ -86,15 +88,140 @@
     return inverse_cells / grid_cells
 
 
-def gram_parts(left, right):
-    left_real = left[:, :, 0].reshape(left.shape[0], -1)
-    left_imag = left[:, :, 1].reshape(left.shape[0], -1)
-    right_real = right[:, :, 0].reshape(right.shape[0], -1)
-    right_imag = right[:, :, 1].reshape(right.shape[0], -1)
-    inner_product = partial(jnp.einsum, "km,jm->kj", precision=HIGHEST)
-    real_sum = inner_product(left_real, right_real) + inner_product(left_imag, right_imag)
-    imag_sum = inner_product(left_real, right_imag) - inner_product(left_imag, right_real)
-    return (real_sum, imag_sum)
+def depth_step(shape):
+    depth = shape[3]
+    step = depth
+    plane = 4 * math.prod(shape[:3]) * math.prod(shape[4:])
+    while step % 2 == 0 and step * plane > (1 << 20):
+        step //= 2
+    return step
+
+
+def block_spec(shape, step):
+    return pl.BlockSpec(shape[:3] + (step,) + shape[4:], lambda d: (0, 0, 0, d, 0, 0))
+
+
+def gram_kernel(plan, step, *refs):
+    *inputs, out = refs
+    rows, lanes = inputs[0].shape[4:]
+
+    @pl.when(pl.program_id(0) == 0)
+    def _():
+        out[...] = jnp.zeros_like(out)
+
+    base = 0
+    for (left, left_band), rights in plan:
+
+        def body(depth, sums, left=left, left_band=left_band, rights=rights):
+            sums = list(sums)
+            for row in range(0, rows, 8):
+                for lane in range(0, lanes, 128):
+                    tile = (depth, pl.ds(row, 8), pl.ds(lane, 128))
+                    for comp in range(2):
+                        left_real = inputs[left][(left_band, comp, 0) + tile]
+                        left_imag = inputs[left][(left_band, comp, 1) + tile]
+                        for place, (right, right_band) in enumerate(rights):
+                            right_real = inputs[right][(right_band, comp, 0) + tile]
+                            right_imag = inputs[right][(right_band, comp, 1) + tile]
+                            sums[2 * place] += left_real * right_real + left_imag * right_imag
+                            sums[2 * place + 1] += left_real * right_imag - left_imag * right_real
+            return tuple(sums)
+
+        zeros = tuple(jnp.zeros((8, 128), jnp.float32) for _ in range(2 * len(rights)))
+        sums = lax.fori_loop(0, step, body, zeros)
+        for place, value in enumerate(sums):
+            out[base + place] += value
+        base += 2 * len(rights)
+
+
+def gram_sums(arrays, pairs):
+    shape = arrays[0].shape
+    bands = shape[0]
+    step = depth_step(shape)
+    plan = []
+    for left in sorted({left for left, _ in pairs}):
+        for band in range(bands):
+            rights = [(r, j) for l, r in pairs if l == left for j in range(bands)]
+            plan.append(((left, band), rights))
+    count = sum(2 * len(rights) for _, rights in plan)
+    cells = math.prod(shape[3:])
+    sums = pl.pallas_call(
+        partial(gram_kernel, plan, step),
+        grid=(shape[3] // step,),
+        in_specs=[block_spec(shape, step) for _ in arrays],
+        out_specs=pl.BlockSpec((count, 8, 128), lambda d: (0, 0, 0)),
+        out_shape=jax.ShapeDtypeStruct((count, 8, 128), jnp.float32),
+        cost_estimate=pl.CostEstimate(
+            flops=8 * count * cells,
+            bytes_accessed=4 * len(arrays) * math.prod(shape),
+            transcendentals=0,
+        ),
+    )(*arrays)
+    sums = jnp.sum(sums, axis=(1, 2))
+    order = []
+    for left in sorted({left for left, _ in pairs}):
+        order.append([p for p in pairs if p[0] == left])
+    found = {}
+    base = 0
+    for group in order:
+        size = bands * len(group) * bands * 2
+        part = sums[base : base + size].reshape(bands, len(group), bands, 2)
+        for place, pair in enumerate(group):
+            found[pair] = part[:, place]
+        base += size
+    return [found[pair] for pair in pairs]
+
+
+def residual_kernel(mixing, block, image, weight, out):
+    bands, _, _, step, rows, lanes = block.shape
+
+    @pl.loop(0, step)
+    def _(depth):
+        for row in range(0, rows, 8):
+            for lane in range(0, lanes, 128):
+                tile = (depth, pl.ds(row, 8), pl.ds(lane, 128))
+                scale = weight[tile]
+                for comp in range(2):
+                    reals = [block[(i, comp, 0) + tile] for i in range(bands)]
+                    imags = [block[(i, comp, 1) + tile] for i in range(bands)]
+                    for j in range(bands):
+                        real = reals[0] * mixing[0, j] - imags[0] * mixing[bands, j]
+                        imag = reals[0] * mixing[bands, j] + imags[0] * mixing[0, j]
+                        for i in range(1, bands):
+                            real += reals[i] * mixing[i, j] - imags[i] * mixing[bands + i, j]
+                            imag += reals[i] * mixing[bands + i, j] + imags[i] * mixing[i, j]
+                        out[(j, comp, 0) + tile] = (image[(j, comp, 0) + tile] - real) / scale
+                        out[(j, comp, 1) + tile] = (image[(j, comp, 1) + tile] - imag) / scale
+
+
+def residual_block(block, image, mixing, weight):
+    shape = block.shape
+    step = depth_step(shape)
+    spec = block_spec(shape, step)
+    return pl.pallas_call(
+        residual_kernel,
+        grid=(shape[3] // step,),
+        in_specs=[
+            pl.BlockSpec(memory_space=pltpu.SMEM),
+            spec,
+            spec,
+            pl.BlockSpec((step,) + shape[4:], lambda d: (d, 0, 0)),
+        ],
+        out_specs=spec,
+        out_shape=jax.ShapeDtypeStruct(shape, jnp.float32),
+    )(mixing, block, image, weight)
+
+
+def sum_over_devices(values):
+    flat = jnp.concatenate([value.reshape(-1) for value in values])
+    for axis in ("slab", "band"):
+        flat = jnp.sum(lax.all_gather(flat, axis), axis=0)
+    totals = []
+    base = 0
+    for value in values:
+        totals.append(flat[base : base + value.size].reshape(value.shape))
+        base += value.size
+    return totals
 
 
 def shards(band_block, material_grid, inverse_permittivity, bloch_index):
@@ -141,15 +268,13 @@
         return slab_operator(points)
 
     image = apply_operator(band_block)
-    correlation_real, correlation_imag = gram_parts(band_block, band_block)
-    cross_real, cross_imag = gram_parts(band_block, image)
-    correlation_real, correlation_imag, cross_real, cross_imag = lax.psum(
-        (correlation_real, correlation_imag, cross_real, cross_imag), ("band", "slab")
-    )
-    correlation_real = correlation_real / grid_cells
-    correlation_imag = correlation_imag / grid_cells
-    cross_real = cross_real / grid_cells
-    cross_imag = cross_imag / grid_cells
+    (own_sum,) = gram_sums([band_block], [(0, 0)])
+    (cross_sum,) = gram_sums([band_block, image], [(0, 1)])
+    own_total, cross_total = sum_over_devices([own_sum, cross_sum])
+    correlation_real = own_total[..., 0] / grid_cells
+    correlation_imag = own_total[..., 1] / grid_cells
+    cross_real = cross_total[..., 0] / grid_cells
+    cross_imag = cross_total[..., 1] / grid_cells
     system = jnp.concatenate(
         [
             jnp.concatenate([correlation_real, -correlation_imag], 1),
@@ -160,33 +285,17 @@
     right_side = jnp.concatenate([cross_real, cross_imag], 0)
     factor = jnp.linalg.cholesky(system)
     solution = jax.scipy.linalg.cho_solve((factor, True), right_side)
-    mixing_real = solution[:band_count]
-    mixing_imag = solution[band_count:]
-    block_real = band_block[:, :, 0]
-    block_imag = band_block[:, :, 1]
-    combine = partial(jnp.einsum, "iabcd,ij->jabcd", precision=HIGHEST)
-    residual_real = image[:, :, 0] - (
-        combine(block_real, mixing_real) - combine(block_imag, mixing_imag)
-    )
-    residual_imag = image[:, :, 1] - (
-        combine(block_real, mixing_imag) + combine(block_imag, mixing_real)
-    )
     magnitude = point_frame[2]
-    search_block = jnp.stack([residual_real, residual_imag], axis=2) / (magnitude * magnitude + 1.0)
+    search_block = residual_block(band_block, image, solution, magnitude * magnitude + 1.0)
     search_image = apply_operator(search_block)
-    stacked = jnp.concatenate([band_block, search_block], 0)
-    joint_real, joint_imag = gram_parts(stacked, search_block)
-    image_real, image_imag = gram_parts(stacked, search_image)
-    back_real, back_imag = gram_parts(search_block, image)
-    joint_real, joint_imag, image_real, image_imag, back_real, back_imag = lax.psum(
-        (joint_real, joint_imag, image_real, image_imag, back_real, back_imag), ("band", "slab")
-    )
-    joint_real = joint_real / grid_cells
-    joint_imag = joint_imag / grid_cells
-    image_real = image_real / grid_cells
-    image_imag = image_imag / grid_cells
-    back_real = back_real / grid_cells
-    back_imag = back_imag / grid_cells
+    early = gram_sums([band_block, search_block, image], [(0, 1), (1, 1), (1, 2)])
+    late = gram_sums([band_block, search_block, search_image], [(0, 2), (1, 2)])
+    totals = [total / grid_cells for total in sum_over_devices(early + late)]
+    joint = jnp.concatenate(totals[:2], 0)
+    across = jnp.concatenate(totals[3:], 0)
+    joint_real, joint_imag = joint[..., 0], joint[..., 1]
+    back_real, back_imag = totals[2][..., 0], totals[2][..., 1]
+    image_real, image_imag = across[..., 0], across[..., 1]
     upper_real = jnp.concatenate([correlation_real, joint_real[:band_count]], 1)
     lower_real = jnp.concatenate([joint_real[:band_count].T, joint_real[band_count:]], 1)
     upper_imag = jnp.concatenate([correlation_imag, joint_imag[:band_count]], 1)

time: 1230 us -> 1090 us (0.89)
  matrix products: 369 us -> 157 us
  waiting for transfers between devices: 173 us -> 242 us
  blocking collectives: 557 us -> 518 us
  Pallas kernels: 0 us -> 38.9 us
    dot_general x24 -> x0, matrix products: 214 us -> none  [the longest x5 51.4 us: gram_parts(): inner_product(left_imag, right_imag)]
    psum x2 -> x0, blocking collectives: 83.8 us -> none  [the longest x1 42 us: shards(): lax.psum((correlation_real, correlation_imag, cross_real, cross_imag), ('...]
    all_to_all x2, waiting for transfers between devices: 0.01 us -> 68.8 us  [slab_operator(): lax.all_to_all(local_image, 'band', split_axis=3, concat_axis=0, tiled=True)]
    unnamed x0 -> x4, blocking collectives: none -> 41.4 us
    pallas_call x0 -> x5, Pallas kernels: none -> 38.9 us  [the longest x4 31.9 us: gram_sums(): pl.pallas_call(partial(gram_kernel, plan, step), grid=(shape[3] // step,)...]
  transfers between devices with their start and end apart: 4 -> 4, of which waited for: 2 -> 4; matrix products, arithmetic and copies ran while one was open for 11% -> 1% of each run, Pallas kernels for 0% -> 2%
where the time goes in v1:
time: 1090 us; the launch traced here: 1070 us
  blocking collectives  518 us (48%)
  waiting for transfers between devices  242 us (22%)
  matrix products  157 us (14%)
  local copies, waits for them, and re-layouts  54 us (5%)
  Pallas kernels  38.9 us (4%)
  other arithmetic  32.5 us (3%)
  starting transfers between devices  22.5 us (2%)
    all_to_all x2, blocking collectives, slab_operator(): lax.all_to_all(transform(spatial, 3, -1.0), 'slab', split_axis=3, concat_...  284 us
    all_to_all x1, blocking collectives, slab_operator(): lax.all_to_all(spectrum, 'slab', split_axis=2, concat_axis=3, tiled=True)  143 us
    all_to_all x1, waiting for transfers between devices, slab_operator(): lax.all_to_all(spectrum, 'slab', split_axis=2, concat_axis=3, tiled=True)  129 us
    dot_general x24, matrix products, transform(): new_real = contract(real_part, cosine) - contract(imaginary, sine_table)  77.9 us
    dot_general x24, matrix products, transform(): new_imag = contract(real_part, sine_table) + contract(imaginary, cosine)  77.9 us
    all_to_all x2, waiting for transfers between devices, slab_operator(): lax.all_to_all(local_image, 'band', split_axis=3, concat_axis=0, tiled=True)  68.8 us
    all_to_all x1, blocking collectives, slab_operator(): lax.all_to_all(points, 'band', split_axis=0, concat_axis=3, tiled=True)  49.5 us
    all_to_all x1, waiting for transfers between devices, slab_operator(): lax.all_to_all(points, 'band', split_axis=0, concat_axis=3, tiled=True)  44 us
  transfers between devices with their start and end apart: 4, of which 4 were waited for; matrix products, arithmetic and copies ran while one was open for 1% of the time, Pallas kernels for 2%

profile of v1, /device:TPU:10, one launch (start us, length us, event | category | flops | bytes accessed | tf_op | source)
XLA Modules:
  0.0 1069.9 jit_solution(14981195007168674051)
XLA Ops:
  0.6 5.4 all-to-all-start
  9.1 44.0 %all-to-all-done = f32[4,2,2,32,16,128]{5,4,3,2,1,0:T(8,128)} async-done(((f32[4,2,2,32,16,128]{5,4,3,2,1,0:T(8,128)}), f32[4,2,2,32,16,128]{5,4,3,2,1,0:T(8,128)}, u32[]{:S(2)}, u32[]{:S(2)}) %all-to-all-start) | async-done | bytes 4194336 | tf_op jit(solution)/shard_map/all_to_all | solution.py:248
  53.1 3.6 copy.165
  64.4 3.5 fusion.54
  67.9 3.2 fusion.116
  77.4 3.4 subtract_bitcast_fusion.7
  80.8 3.3 add_bitcast_fusion.7
  84.9 6.3 copy.170
  91.2 5.6 all-to-all-start.1
  97.5 5.2 add_multiply_fusion.4
  102.7 129.4 %all-to-all-done.1 = f32[3,2,128,16,128]{4,3,0,1,2:T(8,128)} async-done(((f32[3,2,128,16,128]{4,3,0,1,2:T(8,128)}), f32[3,2,128,16,128]{4,3,0,1,2:T(8,128)}, u32[]{:S(2)}, u32[]{:S(2)}) %all-to-all-start.1) | async-done | bytes 6291488 | tf_op jit(solution)/shard_map/all_to_all | solution.py:256
  232.1 3.7 copy.171
  235.8 3.2 fusion.21
  239.1 3.2 fusion.20
  242.3 3.4 subtract_bitcast_fusion.6
  245.7 3.8 add_bitcast_fusion.6
  250.8 3.2 fusion.25
  254.0 3.2 fusion.24
  257.3 3.4 subtract_bitcast_fusion.5
  260.6 3.5 add_bitcast_fusion.5
  265.0 3.6 copy.180
  268.6 142.7 %all_to_all.144 = f32[3,2,16,128,128]{4,2,0,1,3:T(8,128)S(1)} all-to-all(f32[3,2,16,128,128]{4,2,0,1,3:T(8,128)S(1)} %copy.180), channel_id=1, replica_groups=mesh['band'=4,'slab'=8] {'slab'}, dimensions={3} | all-to-all | bytes 12582912 | tf_op jit(solution)/shard_map/all_to_all | solution.py:260
  412.3 3.2 fusion.29
  415.5 3.2 fusion.28
  418.8 3.3 fusion.53
  422.0 3.4 fusion.10
  428.4 3.3 fusion.52
  441.1 4.4 copy.186
  445.6 5.5 all-to-all-start.3
  453.6 5.4 shard_map.67
  461.1 36.7 %all-to-all-done.3 = f32[1,2,2,128,16,128]{5,4,1,2,0,3:T(8,128)} async-done(((f32[1,2,2,128,16,128]{5,4,1,2,0,3:T(8,128)}), f32[1,2,2,128,16,128]{5,4,1,2,0,3:T(8,128)}, u32[]{:S(2)}, u32[]{:S(2)}) %all-to-all-start.3) | async-done | bytes 4194336 | tf_op jit(solution)/shard_map/all_to_all | solution.py:265
  497.8 4.6 copy.307
  502.4 6.2 shard_map.68
  510.0 12.5 %all-reduce = f32[512]{0:T(512)S(1)} all-reduce(f32[512]{0:T(512)S(1)} %maximum_dynamic-update-slice_fusion.1), channel_id=2, replica_groups=mesh['band'=4,'slab'=8] {'slab'}, use_global_device_ids=true, to_apply=%add | all-reduce | flops 512 | bytes 4096
  522.9 8.0 all-reduce.1
  535.7 7.0 shard_map.69.refs_1_
  542.8 49.5 %all_to_all.145 = f32[4,2,2,32,16,128]{5,4,3,2,1,0:T(8,128)S(1)} all-to-all(f32[4,2,2,32,16,128]{5,4,3,2,1,0:T(8,128)} %shard_map.69.refs_1_), channel_id=1, replica_groups=mesh['band'=4,'slab'=8] {'band'}, dimensions={0} | all-to-all | bytes 8388608 | tf_op jit(solution)/shard_map/all_to_all | solution.py:248
  605.1 3.6 fusion.99
  615.0 3.3 subtract_bitcast_fusion.3
  618.2 3.4 add_bitcast_fusion.3
  622.3 3.6 copy.203
  625.9 143.2 %all_to_all.146 = f32[3,2,128,16,128]{4,3,0,1,2:T(8,128)S(1)} all-to-all(f32[3,2,128,16,128]{4,3,0,1,2:T(8,128)S(1)} %copy.203), channel_id=1, replica_groups=mesh['band'=4,'slab'=8] {'slab'}, dimensions={2} | all-to-all | bytes 12582912 | tf_op jit(solution)/shard_map/all_to_all | solution.py:256
  770.1 3.2 fusion.37
  776.5 3.3 subtract_bitcast_fusion.2
  779.8 3.8 add_bitcast_fusion.2
  784.6 3.2 fusion.41
  787.8 3.2 fusion.40
  791.0 3.3 subtract_bitcast_fusion.1
  794.3 3.5 add_bitcast_fusion.1
  798.3 3.6 copy.213
  801.9 141.4 %all_to_all.147 = f32[3,2,16,128,128]{4,2,0,1,3:T(8,128)S(1)} all-to-all(f32[3,2,16,128,128]{4,2,0,1,3:T(8,128)S(1)} %copy.213), channel_id=1, replica_groups=mesh['band'=4,'slab'=8] {'slab'}, dimensions={3} | all-to-all | bytes 12582912 | tf_op jit(solution)/shard_map/all_to_all | solution.py:260
  944.3 3.2 fusion.45
  947.6 3.2 fusion.44
  950.8 3.3 fusion.49
  954.1 3.4 fusion.2
  960.4 3.3 fusion.48
  972.9 4.4 copy.219
  977.3 5.9 all-to-all-start.7
  984.5 11.1 %shard_map.70 = f32[96,8,128]{2,1,0:T(8,128)} custom-call(f32[4,2,2,32,16,128]{5,4,3,2,1,0:T(8,128)} %refs_0_.7, f32[4,2,2,32,16,128]{5,4,3,2,1,0:T(8,128)} %shard_map.69.refs_1_, f32[4,2,2,32,16,128]{5,4,3,2,1,0:T(8,128)} %bitcast.408), custom_call_target="tpu_custom_call" | custom-call | flops 50331648 | bytes 12582912 | tf_op jit(solution)/shard_map/pallas_call | solution.py:148
  997.8 32.1 %all-to-all-done.7 = f32[1,2,2,128,16,128]{5,4,1,2,0,3:T(8,128)} async-done(((f32[1,2,2,128,16,128]{5,4,1,2,0,3:T(8,128)}), f32[1,2,2,128,16,128]{5,4,1,2,0,3:T(8,128)}, u32[]{:S(2)}, u32[]{:S(2)}) %all-to-all-start.7) | async-done | bytes 4194336 | tf_op jit(solution)/shard_map/all_to_all | solution.py:265
  1029.9 4.6 copy.306
  1034.5 9.1 shard_map.71
  1045.3 12.8 %all-reduce.2 = f32[1280]{0:T(1024)S(1)} all-reduce(f32[1280]{0:T(1024)S(1)} %maximum_dynamic-update-slice_fusion), channel_id=4, replica_groups=mesh['band'=4,'slab'=8] {'slab'}, use_global_device_ids=true, to_apply=%add.2 | all-reduce | flops 1280 | bytes 10240
  1058.4 8.0 all-reduce.3
  (133 shorter events, 88.3 us)
Async XLA Ops:
  0.6 52.5 %all-to-all-start = ((f32[4,2,2,32,16,128]{5,4,3,2,1,0:T(8,128)}), f32[4,2,2,32,16,128]{5,4,3,2,1,0:T(8,128)}, u32[]{:S(2)}, u32[]{:S(2)}) async-start(f32[4,2,2,32,16,128]{5,4,3,2,1,0:T(8,128)} %refs_0_.7), calls=%async_computation | async-start | bytes 8388608 | tf_op jit(solution)/shard_map/all_to_all | solution.py:248
  53.1 3.6 copy-start
  91.2 5.7 copy-start.7
  91.2 140.9 %all-to-all-start.1 = ((f32[3,2,128,16,128]{4,3,0,1,2:T(8,128)}), f32[3,2,128,16,128]{4,3,0,1,2:T(8,128)}, u32[]{:S(2)}, u32[]{:S(2)}) async-start(f32[3,2,128,16,128]{4,3,0,1,2:T(8,128)} %copy.170), calls=%async_computation.1 | async-start | bytes 12582912 | tf_op jit(solution)/shard_map/all_to_all | solution.py:256
  245.7 3.8 copy-start.5
  437.8 1.2 copy-start.1
  437.8 1.5 copy-start.3
  445.6 5.5 copy-start.9
  445.6 6.1 copy-start.8
  445.6 52.2 %all-to-all-start.3 = ((f32[1,2,2,128,16,128]{5,4,1,2,0,3:T(8,128)}), f32[1,2,2,128,16,128]{5,4,1,2,0,3:T(8,128)}, u32[]{:S(2)}, u32[]{:S(2)}) async-start(f32[1,2,2,128,16,128]{5,4,1,2,0,3:T(8,128)} %copy.186), calls=%async_computation.3 | async-start | bytes 8388608 | tf_op jit(solution)/shard_map/all_to_all | solution.py:265
  592.7 1.2 copy-start.2
  779.8 3.9 copy-start.6
  969.9 1.2 copy-start.4
  977.3 52.6 %all-to-all-start.7 = ((f32[1,2,2,128,16,128]{5,4,1,2,0,3:T(8,128)}), f32[1,2,2,128,16,128]{5,4,1,2,0,3:T(8,128)}, u32[]{:S(2)}, u32[]{:S(2)}) async-start(f32[1,2,2,128,16,128]{5,4,1,2,0,3:T(8,128)} %copy.219), calls=%async_computation.7 | async-start | bytes 8388608 | tf_op jit(solution)/shard_map/all_to_all | solution.py:265
